TPU v7x, 32 devices: a whole 2x2x4 slice. The times are simulated.
32 devices in a mesh: exp: 8 (over z, x), seq: 4 (over y, core).
Axes of the slice: x: 2, y: 2, z: 4, core: 2. Of those that a mesh axis runs over, the one named last changes fastest.
Arguments:
- out_grad: bfloat16 [4096, 4096], P(('exp', 'seq')), may hold values from -1.5 to 1.5
- chosen: int32 [8, 1024], P('exp'), may hold values from 0 to 4095, as said below
- scores: float32 [8, 1024], P('exp'), may hold values from 0.05 to 1
- saved_pre: bfloat16 [8, 1024, 2, 1536], P('exp', None, None, 'seq'), may hold values from -6 to 6
- gate_up: bfloat16 [8, 4096, 2, 1536], P('exp', None, None, 'seq'), may hold values from -0.09375 to 0.09375
- down: bfloat16 [8, 1536, 4096], P('exp', 'seq'), may hold values from -0.15625 to 0.15625
Outputs:
- in_grad: bfloat16 [4096, 4096], P(('exp', 'seq'))
- score_grad: float32 [8, 1024], P('exp')
Inputs may be any that keep to these rules, and one draw needn't show every extreme that they name: `chosen`: each row lists 1024 different tokens. At most 144 of one row's tokens lie in one block of 512 consecutive tokens (the tokens of one index of exp), and every row has exactly 144 in some block.
All inputs are finite; a program needn't handle non-finite values.
Results may differ from a plain program's by a relative error of at most 0.012.
Values may be sent and summed in bfloat16 or wider, within the bound.
A program may use at most 128 MiB of HBM per device.

v0:
```python
import jax
import jax.numpy as jnp
from jax import lax
from jax.sharding import PartitionSpec as P


def local(out_grad, chosen, scores, saved_pre, gate_up, down):
    n_exp = lax.axis_size("exp")
    n_seq = lax.axis_size("seq")
    capacity = chosen.shape[1]
    slot_most = 9 * capacity // (8 * n_exp)
    tok_count = out_grad.shape[0]
    model_width = out_grad.shape[1]
    group_tok = tok_count * n_seq
    pad_rows = n_exp * slot_most
    hidden_part = gate_up.shape[3]
    group_index = lax.axis_index("exp")
    all_ids = lax.all_gather(chosen, "exp", axis=0, tiled=True)
    group_grad = lax.all_gather(out_grad, "seq", axis=0, tiled=True)
    local_ids = all_ids - group_index * group_tok
    inside = (local_ids >= 0) & (local_ids < group_tok)
    slot_rank = jnp.cumsum(inside.astype(jnp.int32), axis=1) - 1
    slot_ids = jnp.arange(slot_most, dtype=jnp.int32)
    picked = inside[:, None, :] & (slot_rank[:, None, :] == slot_ids[None, :, None])
    filled = jnp.any(picked, axis=2).reshape(pad_rows)
    source_row = jnp.sum(jnp.where(picked, local_ids[:, None, :], 0), axis=2).reshape(pad_rows)
    outgoing = jnp.where(filled[:, None], group_grad[source_row], jnp.zeros((), jnp.bfloat16))
    fetched = lax.all_to_all(outgoing, "exp", split_axis=0, concat_axis=0, tiled=True)
    own_ids = chosen[0]
    owner_group = own_ids // group_tok
    owner_hits = (owner_group[:, None] == jnp.arange(n_exp, dtype=jnp.int32)[None, :]).astype(
        jnp.int32
    )
    slot_order = jnp.sum(jnp.cumsum(owner_hits, axis=0) * owner_hits, axis=1) - 1
    position = owner_group * slot_most + slot_order
    down_rows = down[0]
    mixing = gate_up[0].reshape(model_width, 2 * hidden_part)
    pre_padded = jnp.zeros((pad_rows, 2, hidden_part), jnp.bfloat16).at[position].set(saved_pre[0])
    weight_padded = jnp.zeros((pad_rows,), jnp.float32).at[position].set(scores[0])
    back_grad = lax.dot_general(
        fetched, down_rows, (((1,), (1,)), ((), ())), preferred_element_type=jnp.float32
    )
    gate_pre = pre_padded[:, 0].astype(jnp.float32)
    up_pre = pre_padded[:, 1].astype(jnp.float32)
    sigmoid_gate = jax.nn.sigmoid(gate_pre)
    activated = gate_pre * sigmoid_gate
    hidden = (activated * up_pre).astype(jnp.bfloat16)
    hidden = lax.optimization_barrier(hidden)
    score_part = jnp.sum(hidden.astype(jnp.float32) * back_grad, axis=1)
    scaled = weight_padded[:, None] * back_grad
    d_gate = scaled * up_pre * sigmoid_gate * (1.0 + gate_pre * (1.0 - sigmoid_gate))
    d_up = scaled * activated
    d_both = (
        jnp.stack([d_gate, d_up], axis=1)
        .astype(jnp.bfloat16)
        .reshape(fetched.shape[0], 2 * hidden_part)
    )
    partial_value = lax.dot_general(
        d_both, mixing, (((1,), (1,)), ((), ())), preferred_element_type=jnp.float32
    ).astype(jnp.bfloat16)
    partial_value, score_padded = (partial_value, score_part)
    score_part = score_padded[position]
    score_grad = lax.psum(score_part, "seq")[None, :]
    arrived = lax.all_to_all(partial_value, "exp", split_axis=0, concat_axis=0, tiled=True)
    totals = (
        jnp.zeros((group_tok, model_width), jnp.float32)
        .at[source_row]
        .add(arrived.astype(jnp.float32))
    )
    summed = lax.psum_scatter(totals.astype(jnp.bfloat16), "seq", scatter_dimension=0, tiled=True)
    return (summed, score_grad)


def solution(mesh):
    return jax.shard_map(
        local,
        mesh=mesh,
        in_specs=(
            P(("exp", "seq"), None),
            P("exp", None),
            P("exp", None),
            P("exp", None, None, "seq"),
            P("exp", None, None, "seq"),
            P("exp", "seq", None),
        ),
        out_specs=(P(("exp", "seq"), None), P("exp", None)),
        check_vma=False,
    )
```

profile of v0, /device:TPU:0, one launch (start us, length us, event | category | flops | bytes accessed | tf_op | source)
XLA Modules:
  0.0 611.6 jit_solution(15147982498281689753)
XLA Ops:
  7.2 0.0 copy-start
  7.2 0.0 all-gather.3.cloned.1.call-start
  7.2 0.7 all-gather.3.cloned.1.call-update
  7.9 32.5 %all-gather = s32[8,1,1024]{2,1,0:T(1,128)S(1)} all-gather(s32[1,1,1024]{2,1,0:T(1,128)} %bitcast.99), channel_id=1, replica_groups=mesh['exp'=8,'seq'=4] {'exp'}, dimensions={0}, use_global_device_ids=true | all-gather | bytes 36864 | tf_op jit(solution)/shard_map/all_gather | solution.py:18
  40.4 2.3 reduce-window.14
  42.7 0.3 slice_reduce_fusion.1
  43.0 0.2 reduce-window.15
  43.2 0.1 add_bitcast_fusion.1
  43.3 1.1 select_reduce_fusion
  44.3 0.1 reshape.212
  44.5 0.8 fusion.3
  45.3 1.5 all-gather.3.cloned.1.call-done
  46.8 21.1 %gather_fusion = bf16[1152,4096]{1,0:T(8,128)(2,1)} fusion(bf16[512,4096]{1,0:T(8,128)(2,1)} %all-gather.3.cloned.1.call-done, s32[2048]{0:T(1024)S(1)} %pad_clamp_fusion), kind=kCustom, calls=%fused_computation | custom fusion | bytes 18878976 | tf_op jit(solution)/shard_map/gather | solution.py:27
  67.9 8.0 %broadcast_select_fusion = bf16[8,144,4096]{2,1,0:T(8,128)(2,1)} fusion(bf16[8,144,4096]{2,1,0:T(8,128)(2,1)} %bitcast.87, pred[8,144]{1,0:T(8,128)(4,1)S(1)} %fusion.3), kind=kLoop, calls=%fused_computation.8 | loop fusion | flops 4718592 | bytes 18875520 | tf_op jit(solution)/shard_map/jit(_where)/select_n | solution.py:27
  75.9 0.0 copy-start.3
  75.9 5.6 all-to-all-start
  81.6 0.2 reduce-scatter.2.cloned.1.call-start
  81.8 0.0 copy-done.3
  81.8 2.3 reduce-window.16
  84.1 0.3 slice_reduce_fusion
  84.4 0.2 reduce-window.19
  84.6 0.1 add_bitcast_fusion
  84.7 2.3 broadcast_in_dim.54
  87.0 110.2 %scatter_fusion = bf16[1152,2,384]{2,1,0:T(2,128)(2,1)} fusion(bf16[1152,2,384]{2,1,0:T(2,128)(2,1)} %broadcast_in_dim.54, s32[1024]{0:T(1024)S(1)} %bitcast.102, bf16[1024,2,384]{2,1,0:T(2,128)(2,1)} %bitcast.92), kind=kCustom, calls=%fused_computation.3 | custom fusion | bytes 4722688 | tf_op jit(solution)/shard_map/scatter | solution.py:38
  197.2 6.5 %fusion.27 = (bf16[1152,1,384]{2,1,0:T(2,128)(2,1)}, bf16[1152,1,384]{2,1,0:T(2,128)(2,1)}) fusion(bf16[1152,2,384]{2,1,0:T(2,128)(2,1)} %scatter_fusion), kind=kLoop, calls=%fused_computation.76 | loop fusion | bytes 3538944 | tf_op jit(solution)/shard_map/slice | solution.py:44
  203.6 4.9 copy.18
  208.5 4.8 copy.19
  213.3 2.9 fusion.10
  216.2 6.5 %copy.22 = bf16[512,8,2,384]{3,1,2,0:T(8,128)(2,1)} copy(bf16[512,8,2,384]{3,2,1,0:T(2,128)(2,1)} %bitcast.89) | data formatting | bytes 12582912
  222.7 4.5 scatter_custom_fusion
  227.1 60.5 %all-to-all-done = bf16[8,144,4096]{2,1,0:T(8,128)(2,1)} async-done(((bf16[8,144,4096]{2,1,0:T(8,128)(2,1)}), bf16[8,144,4096]{2,1,0:T(8,128)(2,1)}, u32[]{:S(2)}, u32[]{:S(2)}) %all-to-all-start) | async-done | bytes 9437216 | tf_op jit(solution)/shard_map/all_to_all | solution.py:28
  287.6 0.0 copy-done
  287.6 0.0 copy-start.2
  287.6 11.3 %fusion.16 = (bf16[1152,1,384]{0,2,1:T(8,128)(2,1)S(1)}, bf16[1152,1,384]{0,2,1:T(8,128)(2,1)S(1)}, f32[1152]{0:T(1024)S(1)}) fusion(bf16[1152,1,384]{0,2,1:T(8,128)(2,1)} %copy.19, bf16[1152,1,384]{0,2,1:T(8,128)(2,1)} %copy.18, f32[1152]{0:T(1024)S(1)} %scatter_custom_fusion, bf16[1152,384]{0,1:T(8,128)(2,1)} %fusion.10, bf16[1152,4096]{1,0:T(8,128)(2,1)} %bitcast.10, ...), kind=kOutput, calls=%fused_computation.33 | convolution fusion | flops 3632282624 | bytes 17015808 | tf_op jit(solution)/shard_map/dot_general | solution.py:40
  299.0 0.2 pad_maximum_fusion
  299.1 0.0 copy-done.2
  299.2 8.2 %convolution_convert_fusion = bf16[1152,4096]{1,0:T(8,128)(2,1)S(1)} fusion(bf16[1152,768]{0,1:T(8,128)(2,1)S(1)} %bitcast.91, bf16[4096,768]{1,0:T(8,128)(2,1)S(1)} %bitcast.90), kind=kOutput, calls=%fused_computation.7 | convolution fusion | flops 7252475904 | bytes 17498112 | tf_op jit(solution)/shard_map/dot_general | solution.py:58
  307.3 209.2 %all_to_all.18 = bf16[8,144,4096]{2,1,0:T(8,128)(2,1)} all-to-all(bf16[8,144,4096]{2,1,0:T(8,128)(2,1)S(1)} %bitcast.88), channel_id=1, replica_groups=mesh['exp'=8,'seq'=4] {'exp'}, dimensions={0} | all-to-all | bytes 18874368 | tf_op jit(solution)/shard_map/all_to_all | solution.py:64
  516.5 39.5 %scatter_custom_fusion.2 = f32[512,4096]{1,0:T(8,128)} fusion(s32[1152]{0:T(1024)S(1)} %fusion.20, bf16[1152,4096]{1,0:T(8,128)(2,1)} %bitcast.86, f32[]{:T(128)} %constant.17.clone.1), kind=kCustom, calls=%fused_computation.5 | custom fusion | flops 9437184 | bytes 17825796 | tf_op jit(solution)/shard_map/scatter-add | solution.py:68
  556.0 5.9 convert_element_type.56
  561.9 0.0 reduce-scatter.2.cloned.1.call-update
  562.0 0.0 copy-start.1
  562.0 6.2 %gather_fusion.1 = f32[1024]{0:T(1024)S(1)} fusion(f32[1152]{0:T(1024)S(1)} %get-tuple-element.6, s32[1024]{0:T(1024)S(1)} %broadcast_clamp_fusion), kind=kCustom, calls=%fused_computation.1 | custom fusion | bytes 12288 | tf_op jit(solution)/shard_map/gather | solution.py:62
  568.1 6.5 %psum.7 = f32[1,1024]{1,0:T(1,128)} all-reduce(f32[1,1024]{1,0:T(1,128)S(1)} %bitcast.108), channel_id=1, replica_groups=mesh['exp'=8,'seq'=4] {'seq'}, use_global_device_ids=true, to_apply=%region_12.13 | all-reduce | flops 1024 | bytes 8192 | tf_op jit(solution)/shard_map/psum | solution.py:63
  574.7 30.1 %reduce-scatter.2.cloned.1.call-done = bf16[128,4096]{1,0:T(8,128)(2,1)} async-done(((bf16[512,4096]{1,0:T(8,128)(2,1)}), bf16[128,4096]{1,0:T(8,128)(2,1)}) %reduce-scatter.2.cloned.1.call-update) | async-done | bytes 1048592 | tf_op jit(solution)/shard_map/reduce_scatter | solution.py:70
  604.7 0.0 copy-done.1
  (14 shorter events, 0.2 us)
Async XLA Ops:
  7.2 280.5 %copy-start = (bf16[1,384,4096]{2,1,0:T(8,128)(2,1)S(1)}, bf16[1,384,4096]{2,1,0:T(8,128)(2,1)}, u32[]{:S(2)}) copy-start(bf16[1,384,4096]{2,1,0:T(8,128)(2,1)} %param.11) | copy-start | bytes 9437188
  7.2 39.6 %all-gather.3.cloned.1.call-start = ((), (), s32[]{:S(2)}) async-start(), calls=%async_computation.3 | async-start | bytes 5242880 | tf_op jit(solution)/shard_map/all_gather | solution.py:19
  75.9 5.9 copy-start.3
  75.9 211.7 %all-to-all-start = ((bf16[8,144,4096]{2,1,0:T(8,128)(2,1)}), bf16[8,144,4096]{2,1,0:T(8,128)(2,1)}, u32[]{:S(2)}, u32[]{:S(2)}) async-start(bf16[8,144,4096]{2,1,0:T(8,128)(2,1)} %broadcast_select_fusion), calls=%async_computation | async-start | bytes 18874368 | tf_op jit(solution)/shard_map/all_to_all | solution.py:28
  81.6 523.2 %reduce-scatter.2.cloned.1.call-start = ((), (), s32[]{:S(2)}) async-start(), calls=%async_computation.4 | async-start | bytes 5242880 | tf_op jit(solution)/shard_map/reduce_scatter | solution.py:70
  287.6 11.5 %copy-start.2 = (bf16[512,8,2,384]{3,1,2,0:T(8,128)(2,1)S(1)}, bf16[512,8,2,384]{3,1,2,0:T(8,128)(2,1)}, u32[]{:S(2)}) copy-start(bf16[512,8,2,384]{3,1,2,0:T(8,128)(2,1)} %copy.22) | copy-start | bytes 18874372
  562.0 42.8 %copy-start.1 = (bf16[1,384,4096]{2,1,0:T(8,128)(2,1)S(1)}, bf16[1,384,4096]{2,1,0:T(8,128)(2,1)}, u32[]{:S(2)}) copy-start(bf16[1,384,4096]{2,1,0:T(8,128)(2,1)} %param.11) | copy-start | bytes 9437188
Sparse Core Ops, SparseCore 0:
  9.6 37.1 all-gather.2
  562.1 42.6 reduce-scatter.1
where the time goes:
time: 617 us; the launch traced here: 612 us
  blocking collectives  248 us (40%)
  local copies, waits for them, and re-layouts  168 us (27%)
  waiting for transfers between devices  92.8 us (15%)
  other arithmetic  63.5 us (10%)
  matrix products  19.5 us (3%)
  between operations  14.2 us (2%)
    all_to_all x1, blocking collectives, local(): lax.all_to_all(partial_value, 'exp', split_axis=0, concat_axis=0, tiled=T...  209 us
    scatter x1, local copies, waits for them, and re-layouts, local(): jnp.zeros((pad_rows, 2, hidden_part), jnp.bfloat16).at[position]  110 us
    all_to_all x1, waiting for transfers between devices, local(): lax.all_to_all(outgoing, 'exp', split_axis=0, concat_axis=0, tiled=True)  60.5 us
    scatter-add x1, other arithmetic, local(): totals = jnp.zeros((group_tok, model_width), jnp.float32).at[source_row]....  39.5 us
    all_gather x1, blocking collectives, local(): all_ids = lax.all_gather(chosen, 'exp', axis=0, tiled=True)  32.5 us
    reduce_scatter x1, waiting for transfers between devices, local(): lax.psum_scatter(totals.astype(jnp.bfloat16), 'seq', scatter_dimension=0,...  30.1 us
    gather x1, local copies, waits for them, and re-layouts, local(): group_grad[source_row]  21.1 us
    unnamed x13, local copies, waits for them, and re-layouts  16.2 us
  transfers between devices with their start and end apart: 3, of which 3 were waited for; matrix products, arithmetic and copies ran while one was open for 26% of the time, Pallas kernels for 0%

commit v1 on v0

--- a/solution.py
+++ b/solution.py
@@ -2,6 +2,29 @@
 import jax.numpy as jnp
 from jax import lax
 from jax.sharding import PartitionSpec as P
+
+
+def in_blocks(x, dim, length):
+    lengths = x.shape
+    pieces = x.reshape(*lengths[:dim], length, lengths[dim] // length, *lengths[dim + 1 :])
+    return jnp.moveaxis(pieces, dim, 0)
+
+
+def in_order(parts, dim):
+    shape = list(parts.shape[1:])
+    shape[dim] *= parts.shape[0]
+    return jnp.moveaxis(parts, 0, dim).reshape(shape)
+
+
+def swapped_with_each(array, axis, split_dim, concat_dim):
+    length, index = (lax.axis_size(axis), lax.axis_index(axis))
+    blocks = in_blocks(array, split_dim, length)
+    gathered = [blocks[index]]
+    for step in range(1, length):
+        sent = blocks[index ^ step]
+        gathered.append(lax.ppermute(sent, axis, [(i, i ^ step) for i in range(length)]))
+    blocks = jnp.stack(gathered)[index ^ jnp.arange(length)]
+    return in_order(blocks, concat_dim)
 
 
 def local(out_grad, chosen, scores, saved_pre, gate_up, down):
@@ -25,7 +48,7 @@
     filled = jnp.any(picked, axis=2).reshape(pad_rows)
     source_row = jnp.sum(jnp.where(picked, local_ids[:, None, :], 0), axis=2).reshape(pad_rows)
     outgoing = jnp.where(filled[:, None], group_grad[source_row], jnp.zeros((), jnp.bfloat16))
-    fetched = lax.all_to_all(outgoing, "exp", split_axis=0, concat_axis=0, tiled=True)
+    fetched = swapped_with_each(outgoing, "exp", 0, 0)
     own_ids = chosen[0]
     owner_group = own_ids // group_tok
     owner_hits = (owner_group[:, None] == jnp.arange(n_exp, dtype=jnp.int32)[None, :]).astype(

time: 617 us -> 762 us (1.24)
  waiting for transfers between devices: 92.8 us -> 174 us
  blocking collectives: 248 us -> 280 us
  local copies, waits for them, and re-layouts: 168 us -> 190 us
    ppermute x0 -> x7, waiting for transfers between devices: none -> 142 us  [swapped_with_each(): lax.ppermute(sent, axis, [(i, i ^ step) for i in range(length)])]
    all_to_all x1 -> x0, waiting for transfers between devices: 60.5 us -> none  [local(): lax.all_to_all(outgoing, 'exp', split_axis=0, concat_axis=0, tiled=True)]
    all_to_all x1, blocking collectives: 209 us -> 241 us  [local(): lax.all_to_all(partial_value, 'exp', split_axis=0, concat_axis=0, tiled=T...]
    ppermute x0 -> x7, starting transfers between devices: none -> 13.2 us  [swapped_with_each(): lax.ppermute(sent, axis, [(i, i ^ step) for i in range(length)])]
    gather x0 -> x1, local copies, waits for them, and re-layouts: none -> 8.89 us  [swapped_with_each(): blocks = jnp.stack(gathered)[index ^ jnp.arange(length)]]
    unnamed x13 -> x21, local copies, waits for them, and re-layouts: 16.2 us -> 24.2 us
  transfers between devices with their start and end apart: 3 -> 9, of which waited for: 3 -> 4; matrix products, arithmetic and copies ran while one was open for 26% -> 21% of each run, Pallas kernels for 0% -> 0%
where the time goes in v1:
time: 762 us; the launch traced here: 757 us
  blocking collectives  280 us (37%)
  local copies, waits for them, and re-layouts  190 us (25%)
  waiting for transfers between devices  174 us (23%)
  other arithmetic  63.6 us (8%)
  matrix products  22.2 us (3%)
  between operations  14.3 us (2%)
  starting transfers between devices  13.2 us (2%)
    all_to_all x1, blocking collectives, local(): lax.all_to_all(partial_value, 'exp', split_axis=0, concat_axis=0, tiled=T...  241 us
    ppermute x7, waiting for transfers between devices, swapped_with_each(): lax.ppermute(sent, axis, [(i, i ^ step) for i in range(length)])  142 us
    scatter x1, local copies, waits for them, and re-layouts, local(): jnp.zeros((pad_rows, 2, hidden_part), jnp.bfloat16).at[position]  110 us
    scatter-add x1, other arithmetic, local(): totals = jnp.zeros((group_tok, model_width), jnp.float32).at[source_row]....  39.5 us
    all_gather x1, blocking collectives, local(): all_ids = lax.all_gather(chosen, 'exp', axis=0, tiled=True)  32.5 us
    reduce_scatter x1, waiting for transfers between devices, local(): lax.psum_scatter(totals.astype(jnp.bfloat16), 'seq', scatter_dimension=0,...  31.2 us
    unnamed x21, local copies, waits for them, and re-layouts  24.2 us
    gather x1, local copies, waits for them, and re-layouts, local(): group_grad[source_row]  21.2 us
  transfers between devices with their start and end apart: 9, of which 4 were waited for; matrix products, arithmetic and copies ran while one was open for 21% of the time, Pallas kernels for 0%

profile of v1, /device:TPU:0, one launch (start us, length us, event | category | flops | bytes accessed | tf_op | source)
XLA Modules:
  0.0 757.3 jit_solution(6673524989658875625)
XLA Ops:
  7.2 0.7 all-gather.3.cloned.1.call-update
  8.0 32.5 %all-gather = s32[8,1,1024]{2,1,0:T(1,128)S(1)} all-gather(s32[1,1,1024]{2,1,0:T(1,128)} %bitcast.130), channel_id=1, replica_groups=mesh['exp'=8,'seq'=4] {'exp'}, dimensions={0}, use_global_device_ids=true | all-gather | bytes 36864 | tf_op jit(solution)/shard_map/all_gather | solution.py:41
  40.5 2.3 reduce-window.14
  42.8 0.3 slice_reduce_fusion.1
  43.1 0.2 reduce-window.15
  43.3 1.1 select_reduce_fusion
  44.4 0.1 reshape.230
  44.5 2.3 reduce-window.16
  46.8 0.3 slice_reduce_fusion
  47.1 0.2 reduce-window.19
  47.4 2.3 broadcast_in_dim.55
  49.7 110.1 %scatter_fusion = bf16[1152,2,384]{2,1,0:T(2,128)(2,1)} fusion(bf16[1152,2,384]{2,1,0:T(2,128)(2,1)} %broadcast_in_dim.55, s32[1024]{0:T(1024)S(1)} %bitcast.133, bf16[1024,2,384]{2,1,0:T(2,128)(2,1)} %bitcast.123), kind=kCustom, calls=%fused_computation.4 | custom fusion | bytes 4722688 | tf_op jit(solution)/shard_map/scatter | solution.py:61
  159.8 0.8 fusion.3
  160.6 21.2 %gather_fusion = bf16[1152,4096]{1,0:T(8,128)(2,1)} fusion(bf16[512,4096]{1,0:T(8,128)(2,1)} %all-gather.3.cloned.1.call-done, s32[2048]{0:T(1024)S(1)} %pad_clamp_fusion), kind=kCustom, calls=%fused_computation | custom fusion | bytes 18878976 | tf_op jit(solution)/shard_map/gather | solution.py:50
  181.8 8.0 %broadcast_select_fusion = bf16[8,144,4096]{2,1,0:T(8,128)(2,1)} fusion(bf16[8,144,4096]{2,1,0:T(8,128)(2,1)} %bitcast.117, pred[8,144]{1,0:T(8,128)(4,1)S(1)} %fusion.3), kind=kLoop, calls=%fused_computation.9 | loop fusion | flops 4718592 | bytes 18875520 | tf_op jit(solution)/shard_map/jit(_where)/select_n | solution.py:50
  189.8 7.5 dynamic-slice_bitcast_fusion
  197.3 1.5 collective-permute-start
  198.9 3.7 fusion.28
  202.5 4.8 copy.18
  207.3 4.8 copy.19
  212.1 2.9 fusion.10
  215.0 6.5 copy.22
  221.5 4.5 scatter_custom_fusion
  226.1 2.0 collective-permute-start.2
  228.1 2.1 collective-permute-start.3
  230.2 1.8 collective-permute-start.4
  232.0 3.4 collective-permute-start.5
  235.4 2.4 bitcast_dynamic-update-slice_fusion.6
  237.8 58.3 %collective-permute-done.1 = bf16[144,4096]{1,0:T(8,128)(2,1)S(1)} collective-permute-done((bf16[144,4096]{1,0:T(8,128)(2,1)}, bf16[144,4096]{1,0:T(8,128)(2,1)S(1)}, u32[]{:S(2)}, u32[]{:S(2)}) %collective-permute-start.1) | collective-permute-done | bytes 1179680 | tf_op jit(solution)/shard_map/ppermute | solution.py:25
  296.1 2.3 collective-permute-start.6
  298.4 1.1 bitcast_dynamic-update-slice_fusion.5
  299.5 19.5 %collective-permute-done.2 = bf16[144,4096]{1,0:T(8,128)(2,1)S(1)} collective-permute-done((bf16[144,4096]{1,0:T(8,128)(2,1)}, bf16[144,4096]{1,0:T(8,128)(2,1)S(1)}, u32[]{:S(2)}, u32[]{:S(2)}) %collective-permute-start.2) | collective-permute-done | bytes 1179680 | tf_op jit(solution)/shard_map/ppermute | solution.py:25
  319.0 1.1 bitcast_dynamic-update-slice_fusion.4
  320.1 1.2 bitcast_dynamic-update-slice_fusion.3
  321.3 64.2 %collective-permute-done.4 = bf16[144,4096]{1,0:T(8,128)(2,1)S(1)} collective-permute-done((bf16[144,4096]{1,0:T(8,128)(2,1)}, bf16[144,4096]{1,0:T(8,128)(2,1)S(1)}, u32[]{:S(2)}, u32[]{:S(2)}) %collective-permute-start.4) | collective-permute-done | bytes 1179680 | tf_op jit(solution)/shard_map/ppermute | solution.py:25
  385.5 1.1 bitcast_dynamic-update-slice_fusion.2
  386.6 1.1 bitcast_dynamic-update-slice_fusion.1
  387.7 1.2 bitcast_dynamic-update-slice_fusion
  388.9 8.9 %gather_fusion.1 = bf16[8,144,4096]{2,1,0:T(8,128)(2,1)} fusion(bf16[8,144,4096]{2,1,0:T(8,128)(2,1)} %bitcast_dynamic-update-slice_fusion, s32[1024]{0:T(1024)S(1)} %pad_clamp_fusion.1), kind=kCustom, calls=%fused_computation.1 | custom fusion | bytes 18874400 | tf_op jit(solution)/shard_map/gather | solution.py:26
  397.8 11.2 %fusion.16 = (bf16[1152,1,384]{0,2,1:T(8,128)(2,1)S(1)}, bf16[1152,1,384]{0,2,1:T(8,128)(2,1)S(1)}, f32[1152]{0:T(1024)S(1)}) fusion(bf16[1152,1,384]{0,2,1:T(8,128)(2,1)} %copy.19, bf16[1152,1,384]{0,2,1:T(8,128)(2,1)} %copy.18, f32[1152]{0:T(1024)S(1)} %scatter_custom_fusion, bf16[1152,384]{0,1:T(8,128)(2,1)} %fusion.10, ...), kind=kOutput, calls=%fused_computation.49 | convolution fusion | flops 3632282624 | bytes 17015808 | tf_op jit(solution)/shard_map/dot_general | solution.py:63
  409.0 0.2 pad_maximum_fusion
  409.2 11.0 %convolution_convert_fusion = bf16[1152,4096]{1,0:T(8,128)(2,1)S(1)} fusion(bf16[1152,768]{0,1:T(8,128)(2,1)S(1)} %bitcast.122, bf16[4096,768]{1,0:T(8,128)(2,1)} %bitcast.121), kind=kOutput, calls=%fused_computation.8 | convolution fusion | flops 7252475904 | bytes 17498112 | tf_op jit(solution)/shard_map/dot_general | solution.py:81
  420.2 241.2 %all_to_all.9 = bf16[8,144,4096]{2,1,0:T(8,128)(2,1)} all-to-all(bf16[8,144,4096]{2,1,0:T(8,128)(2,1)S(1)} %bitcast.118), channel_id=1, replica_groups=mesh['exp'=8,'seq'=4] {'exp'}, dimensions={0} | all-to-all | bytes 18874368 | tf_op jit(solution)/shard_map/all_to_all | solution.py:87
  661.4 39.5 %scatter_custom_fusion.2 = f32[512,4096]{1,0:T(8,128)} fusion(s32[1152]{0:T(1024)S(1)} %fusion.20, bf16[1152,4096]{1,0:T(8,128)(2,1)} %bitcast.116, f32[]{:T(128)} %constant.21.clone.1), kind=kCustom, calls=%fused_computation.6 | custom fusion | flops 9437184 | bytes 17825796 | tf_op jit(solution)/shard_map/scatter-add | solution.py:91
  700.8 5.9 convert_element_type.56
  706.8 6.2 gather_fusion.2
  713.0 6.3 psum.7
  719.2 31.2 %reduce-scatter.2.cloned.1.call-done = bf16[128,4096]{1,0:T(8,128)(2,1)} async-done(((bf16[512,4096]{1,0:T(8,128)(2,1)}), bf16[128,4096]{1,0:T(8,128)(2,1)}) %reduce-scatter.2.cloned.1.call-update) | async-done | bytes 1048592 | tf_op jit(solution)/shard_map/reduce_scatter | solution.py:93
  (37 shorter events, 0.6 us)
Async XLA Ops:
  7.2 390.7 %copy-start = (bf16[1,384,4096]{2,1,0:T(8,128)(2,1)S(1)}, bf16[1,384,4096]{2,1,0:T(8,128)(2,1)}, u32[]{:S(2)}) copy-start(bf16[1,384,4096]{2,1,0:T(8,128)(2,1)} %param.11) | copy-start | bytes 9437188
  7.2 37.3 %copy-start.4 = (s32[1,1024]{1,0:T(1,128)S(1)}, s32[1,1024]{1,0:T(1,128)}, u32[]{:S(2)}) copy-start(s32[1,1024]{1,0:T(1,128)} %param.7) | copy-start | bytes 12292
  7.2 153.4 %all-gather.3.cloned.1.call-start = ((), (), s32[]{:S(2)}) async-start(), calls=%async_computation.2 | async-start | bytes 5242880 | tf_op jit(solution)/shard_map/all_gather | solution.py:42
  7.9 742.5 %reduce-scatter.2.cloned.1.call-start = ((), (), s32[]{:S(2)}) async-start(), calls=%async_computation.3 | async-start | bytes 5242880 | tf_op jit(solution)/shard_map/reduce_scatter | solution.py:93
  189.8 9.0 %copy-start.2 = (bf16[1152,2,384]{2,1,0:T(2,128)(2,1)S(1)}, bf16[1152,2,384]{2,1,0:T(2,128)(2,1)}, u32[]{:S(2)}) copy-start(bf16[1152,2,384]{2,1,0:T(2,128)(2,1)} %scatter_fusion) | copy-start | bytes 5308420
  197.3 34.7 %collective-permute-start = (bf16[144,4096]{1,0:T(8,128)(2,1)}, bf16[144,4096]{1,0:T(8,128)(2,1)}, u32[]{:S(2)}, u32[]{:S(2)}) collective-permute-start(bf16[144,4096]{1,0:T(8,128)(2,1)} %get-tuple-element.10), channel_id=1, source_target_pairs={{0,4},{4,0},{8,12},{12,8},{16,20},{20,16},{24,28},{28,24},{1,5},{5... | collective-permute-start | bytes 3538952 | tf_op jit(solution)/shard_map/ppermute | solution.py:25
  226.0 70.2 %copy-start.3 = (bf16[144,4096]{1,0:T(8,128)(2,1)S(1)}, bf16[144,4096]{1,0:T(8,128)(2,1)}, u32[]{:S(2)}) copy-start(bf16[144,4096]{1,0:T(8,128)(2,1)} %get-tuple-element.4) | copy-start | bytes 3538948
  226.0 70.1 %collective-permute-start.1 = (bf16[144,4096]{1,0:T(8,128)(2,1)}, bf16[144,4096]{1,0:T(8,128)(2,1)S(1)}, u32[]{:S(2)}, u32[]{:S(2)}) collective-permute-start(bf16[144,4096]{1,0:T(8,128)(2,1)} %get-tuple-element.9), channel_id=1, source_target_pairs={{0,8},{4,12},{8,0},{12,4},{16,24},{20,28},{24,16},{28,20},{1,9},{5... | collective-permute-start | bytes 3538952 | tf_op jit(solution)/shard_map/ppermute | solution.py:25
  226.1 92.9 %collective-permute-start.2 = (bf16[144,4096]{1,0:T(8,128)(2,1)}, bf16[144,4096]{1,0:T(8,128)(2,1)S(1)}, u32[]{:S(2)}, u32[]{:S(2)}) collective-permute-start(bf16[144,4096]{1,0:T(8,128)(2,1)} %get-tuple-element.8), channel_id=1, source_target_pairs={{0,12},{4,8},{8,4},{12,0},{16,28},{20,24},{24,20},{28,16},{1,13},{... | collective-permute-start | bytes 3538952 | tf_op jit(solution)/shard_map/ppermute | solution.py:25
  228.1 92.0 %collective-permute-start.3 = (bf16[144,4096]{1,0:T(8,128)(2,1)}, bf16[144,4096]{1,0:T(8,128)(2,1)S(1)}, u32[]{:S(2)}, u32[]{:S(2)}) collective-permute-start(bf16[144,4096]{1,0:T(8,128)(2,1)} %get-tuple-element.7), channel_id=1, source_target_pairs={{0,16},{4,20},{8,24},{12,28},{16,0},{20,4},{24,8},{28,12},{1,17},{... | collective-permute-start | bytes 3538952 | tf_op jit(solution)/shard_map/ppermute | solution.py:25
  230.2 155.3 %collective-permute-start.4 = (bf16[144,4096]{1,0:T(8,128)(2,1)}, bf16[144,4096]{1,0:T(8,128)(2,1)S(1)}, u32[]{:S(2)}, u32[]{:S(2)}) collective-permute-start(bf16[144,4096]{1,0:T(8,128)(2,1)} %get-tuple-element.6), channel_id=1, source_target_pairs={{0,20},{4,16},{8,28},{12,24},{16,4},{20,0},{24,12},{28,8},{1,21},{... | collective-permute-start | bytes 3538952 | tf_op jit(solution)/shard_map/ppermute | solution.py:25
  232.0 154.6 %collective-permute-start.5 = (bf16[144,4096]{1,0:T(8,128)(2,1)}, bf16[144,4096]{1,0:T(8,128)(2,1)S(1)}, u32[]{:S(2)}, u32[]{:S(2)}) collective-permute-start(bf16[144,4096]{1,0:T(8,128)(2,1)} %get-tuple-element.5), channel_id=1, source_target_pairs={{0,24},{4,28},{8,16},{12,20},{16,8},{20,12},{24,0},{28,4},{1,25},{... | collective-permute-start | bytes 3538952 | tf_op jit(solution)/shard_map/ppermute | solution.py:25
  296.1 91.6 %collective-permute-start.6 = (bf16[144,4096]{1,0:T(8,128)(2,1)S(1)}, bf16[144,4096]{1,0:T(8,128)(2,1)S(1)}, u32[]{:S(2)}, u32[]{:S(2)}) collective-permute-start(bf16[144,4096]{1,0:T(8,128)(2,1)S(1)} %copy-done.3), channel_id=1, source_target_pairs={{0,28},{4,24},{8,20},{12,16},{16,12},{20,8},{24,4},{28,0},{1,29},{... | collective-permute-start | bytes 3538952 | tf_op jit(solution)/shard_map/ppermute | solution.py:25
  706.8 43.7 %copy-start.1 = (bf16[1,384,4096]{2,1,0:T(8,128)(2,1)S(1)}, bf16[1,384,4096]{2,1,0:T(8,128)(2,1)}, u32[]{:S(2)}) copy-start(bf16[1,384,4096]{2,1,0:T(8,128)(2,1)} %param.11) | copy-start | bytes 9437188
Sparse Core Ops, SparseCore 0:
  9.6 37.1 all-gather.2
  706.9 43.5 reduce-scatter.1
